TPU v7x, 256 devices: a whole 4x4x8 slice. The times are simulated.
256 devices in a mesh: dp: 16 (over z, core), expert: 16 (over y, x).
Axes of the slice: x: 4, y: 4, z: 8, core: 2. Of those that a mesh axis runs over, the one named last changes fastest.
Arguments:
- tokens: bfloat16 [32768, 2048], P(('dp', 'expert')), may hold values from -6 to 6
- expert_ids: int32 [32768, 2], P(('dp', 'expert')), may hold values from 0 to 7, all different within a row; in each aligned block of 128 rows (0 to 127, 128 to 255, ...) at most 40 rows name the same one
- gate_values: bfloat16 [32768, 2], P(('dp', 'expert')), may hold values from 0.19921875 to 0.796875
- w_gate: bfloat16 [16, 2048, 896], P('expert', 'dp'), may hold values from -0.125 to 0.125
- w_up: bfloat16 [16, 2048, 896], P('expert', 'dp'), may hold values from -0.125 to 0.125
- w_down: bfloat16 [16, 896, 2048], P('expert', 'dp'), may hold values from -0.0625 to 0.0625
- cotangent: bfloat16 [32768, 2048], P(('dp', 'expert')), may hold values from -6 to 6
- momentum: bfloat16 [16, 896, 2048], P('expert', 'dp'), may hold values from -4 to 4
- worker_error: bfloat16 [16, 16, 896, 2048], P('dp', 'expert'), may hold values from -2 to 2
- server_error: float32 [16, 896, 2048], P('expert', 'dp'), may hold values from -2 to 2
Outputs:
- outputs: bfloat16 [32768, 2048], P(('dp', 'expert'))
- new_momentum: bfloat16 [16, 896, 2048], P('expert', 'dp')
- new_worker_error: bfloat16 [16, 16, 896, 2048], P('dp', 'expert')
- new_server_error: float32 [16, 896, 2048], P('expert', 'dp')
Inputs may be any that keep to these rules, and one draw needn't show every extreme that they name: `expert_ids`: A token names 2 different experts. Among the 128 tokens of one device at most 40 name the same expert, and some device reaches 40.
All inputs are finite; a program needn't handle non-finite values. Where the computation divides by a largest or mean magnitude, that divisor is 1e-20 or more.
Results may differ from a plain program's by a relative error of at most 0.009.
Values may be sent and summed in bfloat16 or wider, within the bound.
No kernel may reach another device: no remote copies, remote signals or barrier semaphores. Data moves between devices by JAX's collectives and lax.ppermute only.
A program may use at most 128 MiB of HBM per device.

v0:
```python
import jax
import jax.numpy as jnp
import numpy as np
from jax import lax
from jax.sharding import PartitionSpec as P

E = 8
EW = 2
TOP = 2
CAP = 40


def squash(values):
    scale = jnp.mean(jnp.abs(values), axis=-1, keepdims=True) + 1e-06
    return (scale * jnp.tanh(values / scale)).astype(jnp.bfloat16)


def per_device(
    tokens,
    expert_ids,
    gate_values,
    w_gate,
    w_up,
    w_down,
    cotangent,
    momentum,
    worker_error,
    server_error,
):
    n_expert = lax.axis_size("expert")
    n_replica = lax.axis_size("dp")
    tok_count = tokens.shape[0]
    width = tokens.shape[1]
    hidden_units = w_gate.shape[2]
    slots = EW * CAP
    share = n_expert // EW
    flat = expert_ids.reshape(-1)
    onehot = (flat[:, None] == jnp.arange(E, dtype=jnp.int32)[None, :]).astype(jnp.int32)
    ranks = jnp.sum((jnp.cumsum(onehot, axis=0) - onehot) * onehot, axis=1)
    position = jnp.where(flat < EW, flat * CAP + ranks, -1)
    select = (position[None, :] == jnp.arange(slots, dtype=jnp.int32)[:, None]).reshape(
        slots, tok_count, TOP
    )
    dispatch = jnp.any(select, axis=2).astype(jnp.bfloat16)
    combine_w = jnp.sum(jnp.where(select, gate_values.astype(jnp.float32)[None], 0.0), axis=2)
    slot_gates = jnp.sum(combine_w, axis=1).astype(jnp.bfloat16).reshape(EW, CAP)
    peer_owner = np.arange(n_expert) // share
    mix = jnp.asarray((peer_owner[:, None] == np.arange(EW)[None, :]).astype(np.float32)).astype(
        jnp.bfloat16
    )

    def spread(buffer):
        return jnp.take(buffer, jnp.asarray(peer_owner, dtype=jnp.int32), axis=0)

    def slot_rows(source):
        return (
            jnp.dot(dispatch, source, preferred_element_type=jnp.float32)
            .astype(jnp.bfloat16)
            .reshape(EW, CAP, width)
        )

    send_rows = spread(slot_rows(tokens))
    send_gates = spread(slot_gates)
    got_rows, got_gates = (
        lax.all_to_all(send_rows, "expert", split_axis=0, concat_axis=0, tiled=True),
        lax.all_to_all(send_gates, "expert", split_axis=0, concat_axis=0, tiled=True),
    )
    rows = got_rows.reshape(n_expert * CAP, width)
    pieces = (
        lax.all_gather(w_gate, "dp", axis=1, tiled=True),
        lax.all_gather(w_up, "dp", axis=1, tiled=True),
    )
    gate_h = jnp.dot(rows, pieces[0][0], preferred_element_type=jnp.float32)
    up_h = jnp.dot(rows, pieces[1][0], preferred_element_type=jnp.float32)
    hidden = (jax.nn.silu(gate_h) * up_h).astype(jnp.bfloat16)
    down_full, mom_full = (
        lax.all_gather(w_down, "dp", axis=1, tiled=True),
        lax.all_gather(momentum, "dp", axis=1, tiled=True),
    )
    partial_value = jnp.dot(hidden, down_full[0], preferred_element_type=jnp.float32).astype(
        jnp.bfloat16
    )
    returned = lax.all_to_all(
        partial_value.reshape(n_expert, CAP, width),
        "expert",
        split_axis=0,
        concat_axis=0,
        tiled=True,
    )
    expert_sum = jnp.einsum("kcd,ke->ecd", returned, mix, preferred_element_type=jnp.float32)
    outputs = jnp.einsum(
        "pt,pd->td",
        combine_w,
        expert_sum.reshape(slots, width),
        precision=lax.Precision.HIGHEST,
        preferred_element_type=jnp.float32,
    ).astype(jnp.bfloat16)
    got_cot = lax.all_to_all(
        spread(slot_rows(cotangent)), "expert", split_axis=0, concat_axis=0, tiled=True
    )
    dy_rows = got_cot.reshape(n_expert * CAP, width)
    gate_rows = got_gates.reshape(n_expert * CAP).astype(jnp.float32)
    weighted = (hidden.astype(jnp.float32) * gate_rows[:, None]).astype(jnp.bfloat16)
    grad = jnp.einsum("rh,rd->hd", weighted, dy_rows, preferred_element_type=jnp.float32)
    corrected = (
        0.9 * mom_full[0].astype(jnp.float32) + 0.1 * grad + worker_error[0, 0].astype(jnp.float32)
    )
    sent = squash(corrected)
    new_worker = (corrected - sent.astype(jnp.float32)).astype(jnp.bfloat16)[None, None]
    pieces = sent.reshape(n_replica, hidden_units // n_replica, width)
    received = lax.all_to_all(pieces, "dp", split_axis=0, concat_axis=0, tiled=True)
    average = jnp.sum(received.astype(jnp.float32), axis=0) / n_replica
    server_in = average + server_error[0]
    served = squash(server_in)
    new_server = (server_in - served.astype(jnp.float32))[None]
    return (outputs, served[None], new_worker, new_server)


def solution(mesh):
    return jax.shard_map(
        per_device,
        mesh=mesh,
        in_specs=(
            P(("dp", "expert"), None),
            P(("dp", "expert"), None),
            P(("dp", "expert"), None),
            P("expert", "dp", None),
            P("expert", "dp", None),
            P("expert", "dp", None),
            P(("dp", "expert"), None),
            P("expert", "dp", None),
            P("dp", "expert", None, None),
            P("expert", "dp", None),
        ),
        out_specs=(
            P(("dp", "expert"), None),
            P("expert", "dp", None),
            P("dp", "expert", None, None),
            P("expert", "dp", None),
        ),
        check_vma=False,
    )
```

profile of v0, /device:TPU:1, one launch (start us, length us, event | category | flops | bytes accessed | tf_op | source)
XLA Modules:
  0.0 293.4 jit_solution(15084399947835725456)
XLA Ops:
  7.2 0.7 all-gather.5.cloned.1.call-update
  8.0 0.7 all-gather.7.cloned.1.call-update
  8.7 0.7 all-gather.9.cloned.1.call-update
  10.0 0.8 copy.50
  11.0 0.7 convert_element_type.85
  12.8 0.7 compare_select_fusion
  13.7 0.7 pad_clamp_fusion
  15.6 7.6 %all-to-all-start.2 = ((bf16[16,1,40]{2,1,0:T(2,128)(2,1)}), bf16[16,1,40]{2,1,0:T(2,128)(2,1)S(1)}, u32[]{:S(2)}, u32[]{:S(2)}) async-start(bf16[16,1,40]{2,1,0:T(2,128)(2,1)} %copy.55), calls=%async_computation.2 | async-start | bytes 16384 | tf_op jit(solution)/shard_map/all_to_all | solution.py:66
  23.5 2.2 gather_fusion.1
  25.7 3.8 %all-to-all-done.2 = bf16[16,1,40]{2,1,0:T(2,128)(2,1)S(1)} async-done(((bf16[16,1,40]{2,1,0:T(2,128)(2,1)}), bf16[16,1,40]{2,1,0:T(2,128)(2,1)S(1)}, u32[]{:S(2)}, u32[]{:S(2)}) %all-to-all-start.2) | async-done | bytes 1312 | tf_op jit(solution)/shard_map/all_to_all | solution.py:66
  29.5 3.8 %all-to-all-start = ((bf16[16,40,2048]{2,1,0:T(8,128)(2,1)}), bf16[16,40,2048]{2,1,0:T(8,128)(2,1)S(1)}, u32[]{:S(2)}, u32[]{:S(2)}) async-start(bf16[16,40,2048]{2,1,0:T(8,128)(2,1)} %gather_fusion.1), calls=%async_computation | async-start | bytes 5242880 | tf_op jit(solution)/shard_map/all_to_all | solution.py:65
  33.3 1.3 convolution_convert_fusion.1
  34.6 2.2 gather_fusion.2
  36.8 31.5 %all-to-all-done = bf16[16,40,2048]{2,1,0:T(8,128)(2,1)S(1)} async-done(((bf16[16,40,2048]{2,1,0:T(8,128)(2,1)}), bf16[16,40,2048]{2,1,0:T(8,128)(2,1)S(1)}, u32[]{:S(2)}, u32[]{:S(2)}) %all-to-all-start) | async-done | bytes 2621472 | tf_op jit(solution)/shard_map/all_to_all | solution.py:65
  68.3 1.5 copy-done.2
  69.8 5.5 %all-to-all-start.3 = ((bf16[16,40,2048]{2,1,0:T(8,128)(2,1)}), bf16[16,40,2048]{2,1,0:T(8,128)(2,1)S(1)}, u32[]{:S(2)}, u32[]{:S(2)}) async-start(bf16[16,40,2048]{2,1,0:T(8,128)(2,1)} %gather_fusion.2), calls=%async_computation.3 | async-start | bytes 5242880 | tf_op jit(solution)/shard_map/all_to_all | solution.py:98
  75.3 7.2 %fusion.5 = f32[640,896]{1,0:T(8,128)} fusion(bf16[640,2048]{1,0:T(8,128)(2,1)} %bitcast.68, bf16[1,2048,896]{2,1,0:T(8,128)(2,1)} %all-gather.5.cloned.1.call-done), kind=kOutput, calls=%fused_computation.14 | convolution fusion | flops 2348810240 | bytes 8585216 | tf_op jit(solution)/shard_map/dot_general | solution.py:73
  82.5 14.8 %all-gather.7.cloned.1.call-done = bf16[1,2048,896]{2,1,0:T(8,128)(2,1)} async-done(((bf16[1,128,896]{2,1,0:T(8,128)(2,1)}), bf16[1,2048,896]{2,1,0:T(8,128)(2,1)}) %all-gather.7.cloned.1.call-update) | async-done | bytes 3670032 | tf_op jit(solution)/shard_map/all_gather | solution.py:71
  97.3 7.5 %multiply_convert_fusion.2 = bf16[640,896]{1,0:T(8,128)(2,1)} fusion(f32[640,896]{1,0:T(8,128)} %fusion.5, bf16[640,2048]{1,0:T(8,128)(2,1)} %bitcast.69, bf16[1,2048,896]{2,1,0:T(8,128)(2,1)} %all-gather.7.cloned.1.call-done), kind=kOutput, calls=%fused_computation.23 | convolution fusion | flops 2352250880 | bytes 9732096 | tf_op jit(solution)/shard_map/dot_general | solution.py:74
  104.8 35.1 %all-gather.9.cloned.1.call-done = bf16[1,896,2048]{2,1,0:T(8,128)(2,1)} async-done(((bf16[1,56,2048]{2,1,0:T(8,128)(2,1)}), bf16[1,896,2048]{2,1,0:T(8,128)(2,1)}) %all-gather.9.cloned.1.call-update) | async-done | bytes 3670032 | tf_op jit(solution)/shard_map/all_gather | solution.py:77
  139.8 6.8 %fusion.7 = bf16[640,2048]{1,0:T(8,128)(2,1)} fusion(bf16[640,896]{1,0:T(8,128)(2,1)} %multiply_convert_fusion.2, bf16[1,896,2048]{2,1,0:T(8,128)(2,1)} %all-gather.9.cloned.1.call-done), kind=kOutput, calls=%fused_computation.16 | convolution fusion | flops 2350120960 | bytes 7438336 | tf_op jit(solution)/shard_map/dot_general | solution.py:80
  146.6 1.5 copy-done.1
  148.1 6.5 %all-to-all-start.1 = ((bf16[16,40,2048]{2,1,0:T(8,128)(2,1)}), bf16[16,40,2048]{2,1,0:T(8,128)(2,1)S(1)}, u32[]{:S(2)}, u32[]{:S(2)}) async-start(bf16[16,40,2048]{2,1,0:T(8,128)(2,1)} %bitcast.67), calls=%async_computation.1 | async-start | bytes 5242880 | tf_op jit(solution)/shard_map/all_to_all | solution.py:83
  154.8 26.9 %all-gather.11.cloned.1.call-done = bf16[1,896,2048]{2,1,0:T(8,128)(2,1)} async-done(((bf16[1,56,2048]{2,1,0:T(8,128)(2,1)}), bf16[1,896,2048]{2,1,0:T(8,128)(2,1)}) %all-gather.11.cloned.1.call-update) | async-done | bytes 3670032 | tf_op jit(solution)/shard_map/all_gather | solution.py:78
  181.7 8.9 %abs_reduce_fusion = (f32[896]{0:T(1024)S(1)}, f32[896,2048]{1,0:T(8,128)S(1)}) fusion(bf16[1,1,896,2048]{3,2,1,0:T(8,128)(2,1)} %param.24, bf16[640,2048]{1,0:T(8,128)(2,1)} %bitcast.66, bf16[640,896]{1,0:T(8,128)(2,1)} %multiply_convert_fusion.2, f32[640]{0:T(1024)S(1)} %reshape.180, bf16[1,896,2048]{2,1,0:T(8,128)(2,1)} %all-gather.11.cloned.1.call-done), kind=kOutput, calls=%fused_computation.8 | convolution fusion | flops 2365209600 | bytes 18454528 | tf_op jit(solution)/shard_map/rh,rd->hd/dot_general | solution.py:104
  190.6 3.9 %fusion = (bf16[1,1,896,2048]{3,2,1,0:T(8,128)(2,1)}, bf16[896,2048]{1,0:T(8,128)(2,1)}) fusion(f32[896,2048]{1,0:T(8,128)S(1)} %get-tuple-element.12, f32[896]{0:T(1024)S(1)} %multiply_add_fusion), kind=kLoop, calls=%fused_computation.9 | loop fusion | flops 11010048 | bytes 14683648 | tf_op jit(solution)/shard_map/broadcast_in_dim | solution.py:109
  194.7 5.8 %all-to-all-start.4 = ((bf16[16,56,2048]{2,1,0:T(8,128)(2,1)}), bf16[16,56,2048]{2,1,0:T(8,128)(2,1)}, u32[]{:S(2)}, u32[]{:S(2)}) async-start(bf16[16,56,2048]{2,1,0:T(8,128)(2,1)} %bitcast.65), calls=%async_computation.4 | async-start | bytes 7340032 | tf_op jit(solution)/shard_map/all_to_all | solution.py:111
  200.6 3.0 %fusion.10 = f32[2,40,2048]{2,0,1:T(2,128)S(1)} fusion(bf16[16,2,1]{0,1,2:T(2,128)(2,1)S(1)} %copy-done.4, bf16[16,40,2048]{2,1,0:T(8,128)(2,1)S(1)} %all-to-all-done.1), kind=kOutput, calls=%fused_computation.17 | convolution fusion | flops 5242880 | bytes 3276864 | tf_op jit(solution)/shard_map/kcd,ke->ecd/dot_general | solution.py:90
  203.9 1.8 convolution_convert_fusion
  205.8 77.2 %all-to-all-done.4 = bf16[16,56,2048]{2,1,0:T(8,128)(2,1)} async-done(((bf16[16,56,2048]{2,1,0:T(8,128)(2,1)}), bf16[16,56,2048]{2,1,0:T(8,128)(2,1)}, u32[]{:S(2)}, u32[]{:S(2)}) %all-to-all-start.4) | async-done | bytes 3670048 | tf_op jit(solution)/shard_map/all_to_all | solution.py:111
  282.9 2.8 convert_reduce_fusion
  285.9 1.0 convert_subtract_fusion
  (38 shorter events, 4.7 us)
Async XLA Ops:
  7.2 16.0 %copy-start = (bf16[128,2048]{1,0:T(8,128)(2,1)S(1)}, bf16[128,2048]{1,0:T(8,128)(2,1)}, u32[]{:S(2)}) copy-start(bf16[128,2048]{1,0:T(8,128)(2,1)} %param.16) | copy-start | bytes 1572868
  7.2 68.2 %all-gather.5.cloned.1.call-start = ((), (), s32[]{:S(2)}) async-start(), calls=%async_computation.5 | async-start | bytes 3899392 | tf_op jit(solution)/shard_map/all_gather | solution.py:70
  7.9 89.4 %all-gather.7.cloned.1.call-start = ((), (), s32[]{:S(2)}) async-start(), calls=%async_computation.6 | async-start | bytes 3899392 | tf_op jit(solution)/shard_map/all_gather | solution.py:71
  8.7 131.2 %all-gather.9.cloned.1.call-start = ((), (), s32[]{:S(2)}) async-start(), calls=%async_computation.7 | async-start | bytes 3899392 | tf_op jit(solution)/shard_map/all_gather | solution.py:77
  9.4 172.3 %all-gather.11.cloned.1.call-start = ((), (), s32[]{:S(2)}) async-start(), calls=%async_computation.8 | async-start | bytes 3899392 | tf_op jit(solution)/shard_map/all_gather | solution.py:78
  15.6 13.9 %all-to-all-start.2 = ((bf16[16,1,40]{2,1,0:T(2,128)(2,1)}), bf16[16,1,40]{2,1,0:T(2,128)(2,1)S(1)}, u32[]{:S(2)}, u32[]{:S(2)}) async-start(bf16[16,1,40]{2,1,0:T(2,128)(2,1)} %copy.55), calls=%async_computation.2 | async-start | bytes 16384 | tf_op jit(solution)/shard_map/all_to_all | solution.py:66
  29.5 38.8 %all-to-all-start = ((bf16[16,40,2048]{2,1,0:T(8,128)(2,1)}), bf16[16,40,2048]{2,1,0:T(8,128)(2,1)S(1)}, u32[]{:S(2)}, u32[]{:S(2)}) async-start(bf16[16,40,2048]{2,1,0:T(8,128)(2,1)} %gather_fusion.1), calls=%async_computation | async-start | bytes 5242880 | tf_op jit(solution)/shard_map/all_to_all | solution.py:65
  68.3 1.5 copy-start.2
  69.8 76.9 %all-to-all-start.3 = ((bf16[16,40,2048]{2,1,0:T(8,128)(2,1)}), bf16[16,40,2048]{2,1,0:T(8,128)(2,1)S(1)}, u32[]{:S(2)}, u32[]{:S(2)}) async-start(bf16[16,40,2048]{2,1,0:T(8,128)(2,1)} %gather_fusion.2), calls=%async_computation.3 | async-start | bytes 5242880 | tf_op jit(solution)/shard_map/all_to_all | solution.py:98
  146.6 1.5 copy-start.1
  148.1 46.6 %all-to-all-start.1 = ((bf16[16,40,2048]{2,1,0:T(8,128)(2,1)}), bf16[16,40,2048]{2,1,0:T(8,128)(2,1)S(1)}, u32[]{:S(2)}, u32[]{:S(2)}) async-start(bf16[16,40,2048]{2,1,0:T(8,128)(2,1)} %bitcast.67), calls=%async_computation.1 | async-start | bytes 5242880 | tf_op jit(solution)/shard_map/all_to_all | solution.py:83
  194.7 5.8 %copy-start.4 = (bf16[16,2,1]{0,1,2:T(2,128)(2,1)S(1)}, bf16[16,2,1]{0,1,2:T(2,128)(2,1)}, u32[]{:S(2)}) copy-start(bf16[16,2,1]{0,1,2:T(2,128)(2,1)} %constant.104) | copy-start | bytes 196
  194.7 88.2 %all-to-all-start.4 = ((bf16[16,56,2048]{2,1,0:T(8,128)(2,1)}), bf16[16,56,2048]{2,1,0:T(8,128)(2,1)}, u32[]{:S(2)}, u32[]{:S(2)}) async-start(bf16[16,56,2048]{2,1,0:T(8,128)(2,1)} %bitcast.65), calls=%async_computation.4 | async-start | bytes 7340032 | tf_op jit(solution)/shard_map/all_to_all | solution.py:111
  203.9 81.8 %copy-start.3 = (f32[1,56,2048]{2,1,0:T(8,128)S(1)}, f32[1,56,2048]{2,1,0:T(8,128)}, u32[]{:S(2)}) copy-start(f32[1,56,2048]{2,1,0:T(8,128)} %param.25) | copy-start | bytes 1376260
Sparse Core Ops, SparseCore 0:
  9.8 45.3 all-gather.4
  57.1 40.1 all-gather.6
  99.1 40.6 all-gather.8
  141.5 40.1 all-gather.10
where the time goes:
time: 294 us; the launch traced here: 293 us
  waiting for transfers between devices  192 us (65%)
  matrix products  36.6 us (12%)
  starting transfers between devices  29.4 us (10%)
  between operations  13.9 us (5%)
  other arithmetic  10.7 us (4%)
  local copies, waits for them, and re-layouts  10.6 us (4%)
    all_to_all x1, waiting for transfers between devices, per_device(): lax.all_to_all(pieces, 'dp', split_axis=0, concat_axis=0, tiled=True)  77.2 us
    all_gather x1, waiting for transfers between devices, per_device(): lax.all_gather(w_down, 'dp', axis=1, tiled=True)  35.1 us
    all_to_all x1, waiting for transfers between devices, per_device(): lax.all_to_all(send_rows, 'expert', split_axis=0, concat_axis=0, tiled=True)  31.5 us
    all_gather x1, waiting for transfers between devices, per_device(): lax.all_gather(momentum, 'dp', axis=1, tiled=True)  26.9 us
    all_gather x1, waiting for transfers between devices, per_device(): lax.all_gather(w_up, 'dp', axis=1, tiled=True)  14.8 us
    dot_general x1, matrix products, per_device(): jnp.einsum('rh,rd->hd', weighted, dy_rows, preferred_element_type=jnp.flo...  8.87 us
    all_to_all x1, starting transfers between devices, per_device(): lax.all_to_all(send_gates, 'expert', split_axis=0, concat_axis=0, tiled=T...  7.58 us
    dot_general x1, matrix products, per_device(): up_h = jnp.dot(rows, pieces[1][0], preferred_element_type=jnp.float32)  7.46 us
  transfers between devices with their start and end apart: 9, of which 7 were waited for; matrix products, arithmetic and copies ran while one was open for 17% of the time, Pallas kernels for 0%

commit v1 on v0

--- a/solution.py
+++ b/solution.py
@@ -68,7 +68,9 @@
     rows = got_rows.reshape(n_expert * CAP, width)
     pieces = (
         lax.all_gather(w_gate, "dp", axis=1, tiled=True),
-        lax.all_gather(w_up, "dp", axis=1, tiled=True),
+        jnp.concatenate(
+            lax.all_to_all(jnp.stack([w_up] * lax.axis_size("dp")), "dp", 0, 0), axis=1
+        ),
     )
     gate_h = jnp.dot(rows, pieces[0][0], preferred_element_type=jnp.float32)
     up_h = jnp.dot(rows, pieces[1][0], preferred_element_type=jnp.float32)

time: 294 us -> 365 us (1.24)
  blocking collectives: 0 us -> 36.6 us
  waiting for transfers between devices: 192 us -> 224 us
  starting transfers between devices: 29.4 us -> 36.1 us
  matrix products: 36.6 us -> 32.9 us
    all_to_all x1, waiting for transfers between devices: 31.5 us -> 94 us  [per_device(): lax.all_to_all(jnp.stack([w_up] * lax.axis_size('dp')), 'dp', 0, 0)]
    all_to_all x0 -> x1, blocking collectives: none -> 36.6 us  [per_device(): lax.all_to_all(send_rows, 'expert', split_axis=0, concat_axis=0, tiled=True)]
    all_gather x1, waiting for transfers between devices: 35.1 us -> 0.01 us  [per_device(): lax.all_gather(w_down, 'dp', axis=1, tiled=True)]
    all_gather x1, waiting for transfers between devices: 26.9 us -> 0.02 us  [per_device(): lax.all_gather(momentum, 'dp', axis=1, tiled=True)]
    all_to_all x1, waiting for transfers between devices: 0.27 us -> 23.7 us  [per_device(): lax.all_to_all(partial_value.reshape(n_expert, CAP, width), 'expert', spl...]
    all_to_all x1, waiting for transfers between devices: 0.01 us -> 21.5 us  [per_device(): lax.all_to_all(spread(slot_rows(cotangent)), 'expert', split_axis=0, conc...]
    all_gather x1 -> x0, waiting for transfers between devices: 14.8 us -> none  [per_device(): lax.all_gather(w_up, 'dp', axis=1, tiled=True)]
    all_to_all x1, starting transfers between devices: 3.76 us -> 11.2 us  [per_device(): lax.all_to_all(jnp.stack([w_up] * lax.axis_size('dp')), 'dp', 0, 0)]
  transfers between devices with their start and end apart: 9 -> 8, of which waited for: 7 -> 5; matrix products, arithmetic and copies ran while one was open for 17% -> 13% of each run, Pallas kernels for 0% -> 0%
where the time goes in v1:
time: 365 us; the launch traced here: 364 us
  waiting for transfers between devices  224 us (61%)
  blocking collectives  36.6 us (10%)
  starting transfers between devices  36.1 us (10%)
  matrix products  32.9 us (9%)
  between operations  14 us (4%)
  other arithmetic  10.7 us (3%)
  local copies, waits for them, and re-layouts  9.99 us (3%)
    all_to_all x1, waiting for transfers between devices, per_device(): lax.all_to_all(jnp.stack([w_up] * lax.axis_size('dp')), 'dp', 0, 0)  94 us
    all_to_all x1, waiting for transfers between devices, per_device(): lax.all_to_all(pieces, 'dp', split_axis=0, concat_axis=0, tiled=True)  77.2 us
    all_to_all x1, blocking collectives, per_device(): lax.all_to_all(send_rows, 'expert', split_axis=0, concat_axis=0, tiled=True)  36.6 us
    all_to_all x1, waiting for transfers between devices, per_device(): lax.all_to_all(partial_value.reshape(n_expert, CAP, width), 'expert', spl...  23.7 us
    all_to_all x1, waiting for transfers between devices, per_device(): lax.all_to_all(spread(slot_rows(cotangent)), 'expert', split_axis=0, conc...  21.5 us
    all_to_all x1, starting transfers between devices, per_device(): lax.all_to_all(jnp.stack([w_up] * lax.axis_size('dp')), 'dp', 0, 0)  11.2 us
    dot_general x1, matrix products, per_device(): jnp.einsum('rh,rd->hd', weighted, dy_rows, preferred_element_type=jnp.flo...  8.88 us
    all_to_all x1, starting transfers between devices, per_device(): lax.all_to_all(pieces, 'dp', split_axis=0, concat_axis=0, tiled=True)  8.87 us
  transfers between devices with their start and end apart: 8, of which 5 were waited for; matrix products, arithmetic and copies ran while one was open for 13% of the time, Pallas kernels for 0%

profile of v1, /device:TPU:1, one launch (start us, length us, event | category | flops | bytes accessed | tf_op | source)
XLA Modules:
  0.0 364.0 jit_solution(7757475522727023207)
XLA Ops:
  7.2 0.7 all-gather.4.cloned.1.call-update
  8.0 0.7 all-gather.6.cloned.1.call-update
  8.7 0.8 copy.50
  9.7 0.7 convert_element_type.85
  11.5 0.7 compare_select_fusion
  12.4 0.7 pad_clamp_fusion
  13.7 0.6 copy.55
  14.3 7.6 %all-to-all-start.3 = ((bf16[16,1,40]{2,1,0:T(2,128)(2,1)}), bf16[16,1,40]{2,1,0:T(2,128)(2,1)S(1)}, u32[]{:S(2)}, u32[]{:S(2)}) async-start(bf16[16,1,40]{2,1,0:T(2,128)(2,1)} %copy.55), calls=%async_computation.3 | async-start | bytes 16384 | tf_op jit(solution)/shard_map/all_to_all | solution.py:66
  22.2 0.7 gather_fusion.1
  22.9 5.3 %all-to-all-done.3 = bf16[16,1,40]{2,1,0:T(2,128)(2,1)S(1)} async-done(((bf16[16,1,40]{2,1,0:T(2,128)(2,1)}), bf16[16,1,40]{2,1,0:T(2,128)(2,1)S(1)}, u32[]{:S(2)}, u32[]{:S(2)}) %all-to-all-start.3) | async-done | bytes 1312 | tf_op jit(solution)/shard_map/all_to_all | solution.py:66
  28.2 36.6 %all_to_all.31 = bf16[16,40,2048]{2,1,0:T(8,128)(2,1)} all-to-all(bf16[16,40,2048]{2,1,0:T(8,128)(2,1)S(1)} %gather_fusion.1), channel_id=1, replica_groups=mesh['dp'=16,'expert'=16] {'expert'}, dimensions={0} | all-to-all | bytes 5242880 | tf_op jit(solution)/shard_map/all_to_all | solution.py:65
  64.8 2.3 stack.2
  67.2 11.2 %all-to-all-start.1 = ((bf16[16,1,128,896]{3,2,1,0:T(8,128)(2,1)}), bf16[16,1,128,896]{3,2,1,0:T(8,128)(2,1)}, u32[]{:S(2)}, u32[]{:S(2)}) async-start(bf16[16,1,128,896]{3,2,1,0:T(8,128)(2,1)} %stack.2), calls=%async_computation.1 | async-start | bytes 7340032 | tf_op jit(solution)/shard_map/all_to_all | solution.py:72
  78.5 0.7 all-gather.8.cloned.1.call-update
  79.4 2.2 gather_fusion.2
  81.6 94.0 %all-to-all-done.1 = bf16[16,1,128,896]{3,2,1,0:T(8,128)(2,1)} async-done(((bf16[16,1,128,896]{3,2,1,0:T(8,128)(2,1)}), bf16[16,1,128,896]{3,2,1,0:T(8,128)(2,1)}, u32[]{:S(2)}, u32[]{:S(2)}) %all-to-all-start.1) | async-done | bytes 3670048 | tf_op jit(solution)/shard_map/all_to_all | solution.py:72
  175.6 4.2 %all-to-all-start.4 = ((bf16[16,40,2048]{2,1,0:T(8,128)(2,1)}), bf16[16,40,2048]{2,1,0:T(8,128)(2,1)S(1)}, u32[]{:S(2)}, u32[]{:S(2)}) async-start(bf16[16,40,2048]{2,1,0:T(8,128)(2,1)} %gather_fusion.2), calls=%async_computation.4 | async-start | bytes 5242880 | tf_op jit(solution)/shard_map/all_to_all | solution.py:100
  179.8 5.9 %fusion.3 = f32[640,896]{1,0:T(8,128)S(1)} fusion(bf16[640,2048]{1,0:T(8,128)(2,1)} %bitcast.65, bf16[1,2048,896]{2,1,0:T(8,128)(2,1)} %all-gather.4.cloned.1.call-done), kind=kOutput, calls=%fused_computation.12 | convolution fusion | flops 2348810240 | bytes 8585216 | tf_op jit(solution)/shard_map/dot_general | solution.py:75
  185.7 6.1 %multiply_convert_fusion.2 = bf16[640,896]{1,0:T(8,128)(2,1)} fusion(f32[640,896]{1,0:T(8,128)S(1)} %fusion.3, bf16[640,2048]{1,0:T(8,128)(2,1)S(1)} %bitcast.66, bf16[2048,896]{1,0:T(8,128)(2,1)} %bitcast.7), kind=kOutput, calls=%fused_computation.21 | convolution fusion | flops 2352250880 | bytes 9732096 | tf_op jit(solution)/shard_map/dot_general | solution.py:76
  191.8 6.8 %fusion.5 = bf16[640,2048]{1,0:T(8,128)(2,1)} fusion(bf16[640,896]{1,0:T(8,128)(2,1)} %multiply_convert_fusion.2, bf16[1,896,2048]{2,1,0:T(8,128)(2,1)} %all-gather.6.cloned.1.call-done), kind=kOutput, calls=%fused_computation.14 | convolution fusion | flops 2350120960 | bytes 7438336 | tf_op jit(solution)/shard_map/dot_general | solution.py:82
  198.6 21.5 %all-to-all-done.4 = bf16[16,40,2048]{2,1,0:T(8,128)(2,1)S(1)} async-done(((bf16[16,40,2048]{2,1,0:T(8,128)(2,1)}), bf16[16,40,2048]{2,1,0:T(8,128)(2,1)S(1)}, u32[]{:S(2)}, u32[]{:S(2)}) %all-to-all-start.4) | async-done | bytes 2621472 | tf_op jit(solution)/shard_map/all_to_all | solution.py:100
  220.1 1.5 copy-done.1
  221.6 4.1 %all-to-all-start.2 = ((bf16[16,40,2048]{2,1,0:T(8,128)(2,1)}), bf16[16,40,2048]{2,1,0:T(8,128)(2,1)S(1)}, u32[]{:S(2)}, u32[]{:S(2)}) async-start(bf16[16,40,2048]{2,1,0:T(8,128)(2,1)} %bitcast.67), calls=%async_computation.2 | async-start | bytes 5242880 | tf_op jit(solution)/shard_map/all_to_all | solution.py:85
  225.8 8.9 %abs_reduce_fusion = (f32[896]{0:T(1024)S(1)}, f32[896,2048]{1,0:T(8,128)S(1)}) fusion(bf16[1,1,896,2048]{3,2,1,0:T(8,128)(2,1)} %param.24, bf16[640,2048]{1,0:T(8,128)(2,1)} %bitcast.64, bf16[640,896]{1,0:T(8,128)(2,1)} %multiply_convert_fusion.2, f32[640]{0:T(1024)S(1)} %reshape.183, bf16[1,896,2048]{2,1,0:T(8,128)(2,1)} %all-gather.8.cloned.1.call-done), kind=kOutput, calls=%fused_computation.8 | convolution fusion | flops 2365209600 | bytes 18454528 | tf_op jit(solution)/shard_map/rh,rd->hd/dot_general | solution.py:106
  234.7 3.9 %fusion = (bf16[1,1,896,2048]{3,2,1,0:T(8,128)(2,1)}, bf16[896,2048]{1,0:T(8,128)(2,1)}) fusion(f32[896,2048]{1,0:T(8,128)S(1)} %get-tuple-element.12, f32[896]{0:T(1024)S(1)} %multiply_add_fusion), kind=kLoop, calls=%fused_computation.9 | loop fusion | flops 11010048 | bytes 14683648 | tf_op jit(solution)/shard_map/broadcast_in_dim | solution.py:111
  238.6 23.7 %all-to-all-done.2 = bf16[16,40,2048]{2,1,0:T(8,128)(2,1)S(1)} async-done(((bf16[16,40,2048]{2,1,0:T(8,128)(2,1)}), bf16[16,40,2048]{2,1,0:T(8,128)(2,1)S(1)}, u32[]{:S(2)}, u32[]{:S(2)}) %all-to-all-start.2) | async-done | bytes 2621472 | tf_op jit(solution)/shard_map/all_to_all | solution.py:85
  262.3 8.9 %all-to-all-start.5 = ((bf16[16,56,2048]{2,1,0:T(8,128)(2,1)}), bf16[16,56,2048]{2,1,0:T(8,128)(2,1)}, u32[]{:S(2)}, u32[]{:S(2)}) async-start(bf16[16,56,2048]{2,1,0:T(8,128)(2,1)} %bitcast.63), calls=%async_computation.5 | async-start | bytes 7340032 | tf_op jit(solution)/shard_map/all_to_all | solution.py:113
  271.1 3.0 fusion.8
  274.5 1.8 convolution_convert_fusion
  276.3 77.2 %all-to-all-done.5 = bf16[16,56,2048]{2,1,0:T(8,128)(2,1)} async-done(((bf16[16,56,2048]{2,1,0:T(8,128)(2,1)}), bf16[16,56,2048]{2,1,0:T(8,128)(2,1)}, u32[]{:S(2)}, u32[]{:S(2)}) %all-to-all-start.5) | async-done | bytes 3670048 | tf_op jit(solution)/shard_map/all_to_all | solution.py:113
  353.5 2.8 convert_reduce_fusion
  356.5 1.0 convert_subtract_fusion
  (41 shorter events, 3.5 us)
Async XLA Ops:
  7.2 14.7 %copy-start = (bf16[128,2048]{1,0:T(8,128)(2,1)S(1)}, bf16[128,2048]{1,0:T(8,128)(2,1)}, u32[]{:S(2)}) copy-start(bf16[128,2048]{1,0:T(8,128)(2,1)} %param.16) | copy-start | bytes 1572868
  7.2 172.6 %all-gather.4.cloned.1.call-start = ((), (), s32[]{:S(2)}) async-start(), calls=%async_computation.6 | async-start | bytes 3899392 | tf_op jit(solution)/shard_map/all_gather | solution.py:70
  7.9 183.9 %all-gather.6.cloned.1.call-start = ((), (), s32[]{:S(2)}) async-start(), calls=%async_computation.7 | async-start | bytes 3899392 | tf_op jit(solution)/shard_map/all_gather | solution.py:79
  14.3 13.9 %all-to-all-start.3 = ((bf16[16,1,40]{2,1,0:T(2,128)(2,1)}), bf16[16,1,40]{2,1,0:T(2,128)(2,1)S(1)}, u32[]{:S(2)}, u32[]{:S(2)}) async-start(bf16[16,1,40]{2,1,0:T(2,128)(2,1)} %copy.55), calls=%async_computation.3 | async-start | bytes 16384 | tf_op jit(solution)/shard_map/all_to_all | solution.py:66
  22.9 42.0 %copy-start.5 = (bf16[1,128,896]{2,1,0:T(8,128)(2,1)S(1)}, bf16[1,128,896]{2,1,0:T(8,128)(2,1)}, u32[]{:S(2)}) copy-start(bf16[1,128,896]{2,1,0:T(8,128)(2,1)} %param.20) | copy-start | bytes 688132
  67.2 12.0 %copy-start.4 = (bf16[128,2048]{1,0:T(8,128)(2,1)S(1)}, bf16[128,2048]{1,0:T(8,128)(2,1)}, u32[]{:S(2)}) copy-start(bf16[128,2048]{1,0:T(8,128)(2,1)} %param.22) | copy-start | bytes 1572868
  67.2 108.4 %all-to-all-start.1 = ((bf16[16,1,128,896]{3,2,1,0:T(8,128)(2,1)}), bf16[16,1,128,896]{3,2,1,0:T(8,128)(2,1)}, u32[]{:S(2)}, u32[]{:S(2)}) async-start(bf16[16,1,128,896]{3,2,1,0:T(8,128)(2,1)} %stack.2), calls=%async_computation.1 | async-start | bytes 7340032 | tf_op jit(solution)/shard_map/all_to_all | solution.py:72
  78.4 147.4 %all-gather.8.cloned.1.call-start = ((), (), s32[]{:S(2)}) async-start(), calls=%async_computation.8 | async-start | bytes 3899392 | tf_op jit(solution)/shard_map/all_gather | solution.py:80
  175.6 44.5 %all-to-all-start.4 = ((bf16[16,40,2048]{2,1,0:T(8,128)(2,1)}), bf16[16,40,2048]{2,1,0:T(8,128)(2,1)S(1)}, u32[]{:S(2)}, u32[]{:S(2)}) async-start(bf16[16,40,2048]{2,1,0:T(8,128)(2,1)} %gather_fusion.2), calls=%async_computation.4 | async-start | bytes 5242880 | tf_op jit(solution)/shard_map/all_to_all | solution.py:100
  179.8 5.9 %copy-start.2 = (bf16[16,40,2048]{2,1,0:T(8,128)(2,1)S(1)}, bf16[16,40,2048]{2,1,0:T(8,128)(2,1)}, u32[]{:S(2)}) copy-start(bf16[16,40,2048]{2,1,0:T(8,128)(2,1)} %all_to_all.31) | copy-start | bytes 7864324
  220.1 1.5 copy-start.1
  221.6 40.7 %all-to-all-start.2 = ((bf16[16,40,2048]{2,1,0:T(8,128)(2,1)}), bf16[16,40,2048]{2,1,0:T(8,128)(2,1)S(1)}, u32[]{:S(2)}, u32[]{:S(2)}) async-start(bf16[16,40,2048]{2,1,0:T(8,128)(2,1)} %bitcast.67), calls=%async_computation.2 | async-start | bytes 5242880 | tf_op jit(solution)/shard_map/all_to_all | solution.py:85
  262.3 8.9 %copy-start.6 = (bf16[16,2,1]{0,1,2:T(2,128)(2,1)S(1)}, bf16[16,2,1]{0,1,2:T(2,128)(2,1)}, u32[]{:S(2)}) copy-start(bf16[16,2,1]{0,1,2:T(2,128)(2,1)} %constant.104) | copy-start | bytes 196
  262.3 91.2 %all-to-all-start.5 = ((bf16[16,56,2048]{2,1,0:T(8,128)(2,1)}), bf16[16,56,2048]{2,1,0:T(8,128)(2,1)}, u32[]{:S(2)}, u32[]{:S(2)}) async-start(bf16[16,56,2048]{2,1,0:T(8,128)(2,1)} %bitcast.63), calls=%async_computation.5 | async-start | bytes 7340032 | tf_op jit(solution)/shard_map/all_to_all | solution.py:113
  274.5 81.8 %copy-start.3 = (f32[1,56,2048]{2,1,0:T(8,128)S(1)}, f32[1,56,2048]{2,1,0:T(8,128)}, u32[]{:S(2)}) copy-start(f32[1,56,2048]{2,1,0:T(8,128)} %param.25) | copy-start | bytes 1376260
Sparse Core Ops, SparseCore 0:
  9.8 45.3 all-gather.3
  57.1 73.0 all-gather.5
  132.0 61.6 all-gather.7
